TPU v7x, 128 devices: a whole 4x4x4 slice. The times are simulated.
128 devices in a mesh: hi: 16 (over y, x), lo: 8 (over z, core).
Axes of the slice: x: 4, y: 4, z: 4, core: 2. Of those that a mesh axis runs over, the one named last changes fastest.
Arguments:
- previous: float32 [32, 2097152], P(None, ('hi', 'lo')), may hold values from -6 to 6
- current: float32 [32, 2097152], P(None, ('hi', 'lo')), may hold values from -6 to 6
- field_levels: int32 [21], replicated, may hold values from -4 to 4
- bond_levels: int32 [20], replicated, may hold values from 1 to 3
Outputs:
- ortho_block: float32 [32, 2097152], P(None, ('hi', 'lo'))
- upper_factor: float32 [32, 32], replicated
All inputs are finite; a program needn't handle non-finite values.
Results may differ from a plain program's by a relative error of at most 0.00005.
Values sent between devices are 32-bit elements; how exact they have to be, the bound alone decides.
A program may use at most 64 MiB of HBM per device.

v0:
```python
import jax
import jax.numpy as jnp
from jax import lax
from jax.sharding import PartitionSpec as P

FIELD_STEP = 0.75
COUPLING_STEP = 0.5


def chain_matrix(couplings, bit_count, bond_list):
    width = 2**bit_count
    rows = lax.iota(jnp.int32, width)[:, None]
    cols = lax.iota(jnp.int32, width)[None, :]
    matrix = jnp.zeros((width, width), jnp.float32)
    for site_number, spot in bond_list:
        differ = cols >> spot & 1 != cols >> spot + 1 & 1
        target = rows == cols ^ 3 << spot
        matrix = matrix + jnp.where(differ & target, 0.5 * couplings[site_number], 0.0)
    return matrix


def cross_flip(values, coupling, low_spot):
    width = values.shape[-1]
    index = lax.iota(jnp.int32, width)
    permute = (index[:, None] == index[None, :] ^ 1 << low_spot).astype(jnp.float32)
    moved = jnp.einsum("vatbl,lj->vatbj", values, permute, precision=lax.Precision.HIGHEST)
    flipped = jnp.flip(moved, axis=2)
    upper = lax.iota(jnp.int32, 2)[:, None]
    keep = (index[None, :] >> low_spot & 1 != upper).astype(jnp.float32)
    return 0.5 * coupling * flipped * keep[None, None, :, None, :]


def local(previous, current, field_levels, bond_levels):
    vectors, amp_count = current.shape
    site_count = field_levels.shape[0]
    devices = lax.axis_size("hi") * lax.axis_size("lo")
    local_bits = amp_count.bit_length() - 1
    global_bits = devices.bit_length() - 1
    rest_bits = local_bits - global_bits
    device = lax.axis_index("hi") * lax.axis_size("lo") + lax.axis_index("lo")
    local_index = lax.iota(jnp.int32, amp_count)
    top_width = 2**global_bits
    low_width = 2**rest_bits

    def position(site_number):
        if site_number < global_bits:
            return rest_bits + site_number
        return site_number - global_bits

    def spin_value(site_number):
        if site_number < local_bits:
            return 0.5 - (local_index >> position(site_number) & 1).astype(jnp.float32)
        return 0.5 - (device >> site_number - local_bits & 1).astype(jnp.float32)

    fields = FIELD_STEP * field_levels.astype(jnp.float32)
    couplings = COUPLING_STEP * bond_levels.astype(jnp.float32)
    diagonal = jnp.zeros((amp_count,), jnp.float32)
    for site_number in range(site_count):
        diagonal = diagonal + fields[site_number] * spin_value(site_number)
        if site_number < site_count - 1:
            diagonal = diagonal + couplings[site_number] * spin_value(site_number) * spin_value(
                site_number + 1
            )
    top_matrix = chain_matrix(
        couplings,
        global_bits,
        [(site_number, site_number) for site_number in range(global_bits - 1)],
    )
    low_matrix = chain_matrix(
        couplings,
        rest_bits,
        [
            (site_number, site_number - global_bits)
            for site_number in range(global_bits, local_bits - 1)
        ],
    )
    blocks = current.reshape(vectors, top_width, low_width)
    applied = diagonal[None, :] * current
    applied = applied + jnp.einsum(
        "vtl,tu->vul", blocks, top_matrix, precision=lax.Precision.HIGHEST
    ).reshape(vectors, amp_count)
    applied = applied + jnp.einsum(
        "vtl,lu->vtu", blocks, low_matrix, precision=lax.Precision.HIGHEST
    ).reshape(vectors, amp_count)
    joined = cross_flip(
        current.reshape(vectors, 1, 2, top_width // 2, low_width), couplings[global_bits - 1], 0
    )
    applied = applied + joined.reshape(vectors, amp_count)
    far_matrix = chain_matrix(
        couplings,
        global_bits,
        [
            (site_number, site_number - local_bits)
            for site_number in range(local_bits, site_count - 1)
        ],
    )
    shaped = current.reshape(vectors, devices, amp_count // devices)
    arrived = lax.all_to_all(shaped, ("hi", "lo"), split_axis=1, concat_axis=1, tiled=True)
    count = arrived.shape[0]
    bond_terms = jnp.einsum(
        "vtl,tu->vul", arrived, far_matrix, precision=lax.Precision.HIGHEST
    ).reshape(count, amp_count)
    seam = cross_flip(
        arrived.reshape(count, top_width // 2, 2, 1, low_width),
        couplings[local_bits - 1],
        rest_bits - 1,
    )
    bond_terms = bond_terms + seam.reshape(count, amp_count)
    remote_part = lax.all_to_all(
        bond_terms.reshape(arrived.shape), ("hi", "lo"), split_axis=1, concat_axis=1, tiled=True
    ).reshape(vectors, amp_count)
    filtered = 4.0 / site_count * (applied + remote_part) - previous
    local_gram = jnp.dot(filtered, filtered.T, precision=lax.Precision.HIGHEST) / (
        amp_count * devices
    )
    gram_matrix = lax.psum(local_gram, ("hi", "lo"))
    lower_factor = jnp.linalg.cholesky(gram_matrix)
    inverse = jax.scipy.linalg.solve_triangular(
        lower_factor, jnp.eye(vectors, dtype=jnp.float32), lower=True
    )
    ortho_block = jnp.dot(inverse, filtered, precision=lax.Precision.HIGHEST)
    return (ortho_block, lower_factor.T)


def solution(mesh):
    in_specs = (P(None, ("hi", "lo")), P(None, ("hi", "lo")), P(), P())
    out_specs = (P(None, ("hi", "lo")), P())
    return jax.shard_map(local, mesh=mesh, in_specs=in_specs, out_specs=out_specs, check_vma=False)
```

profile of v0, /device:TPU:1, one launch (start us, length us, event | category | flops | bytes accessed | tf_op | source)
XLA Modules:
  0.0 200.1 jit_solution(15617030087911046846)
XLA Ops:
  0.6 3.2 %copy_bitcast_fusion = f32[32,128,128]{2,0,1:T(8,128)} fusion(f32[32,16384]{1,0:T(8,128)} %param.5), kind=kLoop, calls=%fused_computation.6 | loop fusion | bytes 4194304 | tf_op jit(solution)/shard_map/reshape | solution.py:77
  3.8 0.0 copy-start
  3.8 0.0 copy-start.1
  3.8 11.5 %all-to-all-start = ((f32[32,128,128]{2,0,1:T(8,128)}), f32[32,128,128]{2,0,1:T(8,128)S(1)}, u32[]{:S(2)}, u32[]{:S(2)}) async-start(f32[32,128,128]{2,0,1:T(8,128)} %copy_bitcast_fusion), calls=%async_computation | async-start | bytes 4194304 | tf_op jit(solution)/shard_map/all_to_all | solution.py:98
  15.3 0.0 copy-done
  15.4 0.7 fusion.153
  20.4 0.0 copy-done.1
  20.4 25.0 %all-to-all-done = f32[32,128,128]{2,0,1:T(8,128)S(1)} async-done(((f32[32,128,128]{2,0,1:T(8,128)}), f32[32,128,128]{2,0,1:T(8,128)S(1)}, u32[]{:S(2)}, u32[]{:S(2)}) %all-to-all-start) | async-done | bytes 2097184 | tf_op jit(solution)/shard_map/all_to_all | solution.py:98
  45.4 2.3 %fusion.7 = f32[32,64,2,128]{3,1,2,0:T(8,128)S(1)} fusion(f32[32,64,2,128]{3,0,2,1:T(8,128)S(1)} %bitcast.129, s32[128]{0:T(128)S(1)} %iota_xor_fusion), kind=kOutput, calls=%fused_computation.14 | convolution fusion | flops 805322752 | bytes 4194816 | tf_op jit(solution)/shard_map/vatbl,lj->vatbj/dot_general | solution.py:26
  47.7 0.3 multiply_multiply_fusion
  48.1 1.7 copy.31
  49.8 3.2 %bitcast_add_fusion.3 = f32[32,128,128]{2,1,0:T(8,128)S(1)} fusion(f32[32,128,128]{2,1,0:T(8,128)S(1)} %bitcast.133, f32[32,128,128]{2,0,1:T(8,128)S(1)} %all-to-all-done, f32[]{:T(128)S(6)} %mul.670, f32[]{:T(128)S(6)} %mul.669, f32[]{:T(128)S(6)} %mul.668, f32[]{:T(128)S(6)} %mul.667, f32[]{:T(128)S(6)} %mul.666, f32[]{:T(128)S(6)} %mul.665, ...), kind=kOutput, calls=%fused_computation.7 | convolution fusion | flops 806207488 | bytes 6295320 | tf_op jit(solution)/shard_map/vtl,tu->vul/dot_general | solution.py:100
  53.0 2.5 %copy.32 = f32[32,128,128]{2,0,1:T(8,128)} copy(f32[32,128,128]{2,1,0:T(8,128)S(1)} %bitcast_add_fusion.3) | data formatting | bytes 4194304 | tf_op jit(solution)/shard_map/add | solution.py:108
  55.5 5.9 %all-to-all-start.1 = ((f32[32,128,128]{2,0,1:T(8,128)}), f32[32,128,128]{2,0,1:T(8,128)}, u32[]{:S(2)}, u32[]{:S(2)}) async-start(f32[32,128,128]{2,0,1:T(8,128)} %copy.32), calls=%async_computation.1 | async-start | bytes 4194304 | tf_op jit(solution)/shard_map/all_to_all | solution.py:109
  61.4 0.7 fusion.151
  74.1 2.0 copy.42
  76.1 3.4 %convolution_bitcast_fusion.1 = f32[32,128,128]{1,2,0:T(8,128)} fusion(f32[32,128,128]{2,1,0:T(8,128)S(1)} %bitcast.125, f32[]{:T(128)S(6)} %mul.659, f32[]{:T(128)S(6)} %mul.658, f32[]{:T(128)S(6)} %mul.657, f32[]{:T(128)S(6)} %mul.656, f32[]{:T(128)S(6)} %mul.655, f32[]{:T(128)S(6)} %mul.654, s32[128]{0:T(128)S(1)} %get-tuple-element.52, ...), kind=kOutput, calls=%fused_computation.16 | convolution fusion | flops 805683200 | bytes 4198168 | tf_op jit(solution)/shard_map/vtl,lu->vtu/dot_general | solution.py:82
  79.5 2.9 %copy.27 = f32[32,128,128]{2,1,0:T(8,128)} copy(f32[32,128,128]{1,2,0:T(8,128)} %convolution_bitcast_fusion.1) | data formatting | bytes 4194304 | tf_op jit(solution)/shard_map/vtl,lu->vtu/dot_general | solution.py:82
  86.2 0.6 fusion.152
  86.7 17.3 %add_add_fusion = f32[16384]{0:T(1024)S(1)} fusion(f32[]{:T(128)S(6)} %mul.645, f32[]{:T(128)S(6)} %mul.644, f32[]{:T(128)S(6)} %mul.642, f32[]{:T(128)S(6)} %mul.641, f32[]{:T(128)S(6)} %mul.639, f32[]{:T(128)S(6)} %mul.638, f32[]{:T(128)S(6)} %mul.636, f32[]{:T(128)S(6)} %mul.635, f32[]{:T(128)S(6)} %mul.633, f32[]{:T(128)S(6)} %mul.632, f32[]{:T(128)S(6)} %mul.630, ...), kind=kLoop, calls=%fused_computation.63 | loop fusion | flops 2260992 | bytes 65704 | tf_op jit(solution)/shard_map/add | solution.py:59
  104.1 1.1 convolution_bitcast_fusion
  105.2 1.6 multiply_multiply_fusion.1
  106.8 3.4 %fusion.14 = f32[128,32,128]{2,0,1:T(8,128)} fusion(f32[32,128,128]{2,1,0:T(8,128)S(1)} %bitcast.127, f32[]{:T(128)S(6)} %mul.653, s32[128]{0:T(128)S(1)} %get-tuple-element.52, f32[]{:T(128)S(6)} %mul.652, s32[128]{0:T(128)S(1)} %get-tuple-element.53, f32[]{:T(128)S(6)} %mul.651, s32[128]{0:T(128)S(1)} %get-tuple-element.54, f32[]{:T(128)S(6)} %mul.650, ...), kind=kOutput, calls=%fused_computation.20 | convolution fusion | flops 805683200 | bytes 4198168 | tf_op jit(solution)/shard_map/vtl,tu->vul/dot_general | solution.py:79
  110.2 0.0 all-to-all-done.1
  110.2 9.6 %fusion.2 = f32[32,16384]{1,0:T(8,128)S(1)} fusion(f32[32,16384]{1,0:T(8,128)} %param.4, f32[4,8,128,128]{3,2,1,0:T(8,128)} %bitcast.130, f32[4,8,128,128]{3,2,1,0:T(8,128)} %bitcast.132, f32[4,8,128,128]{3,2,1,0:T(8,128)} %bitcast.131, f32[32,16384]{1,0:T(8,128)} %param.5, f32[16384]{0:T(1024)S(1)} %add_add_fusion, f32[32,128,128]{2,0,1:T(8,128)} %all-to-all-done.1), kind=kLoop, calls=%fused_computation.3 | loop fusion | flops 3670016 | bytes 14745600 | tf_op jit(solution)/shard_map/sub | solution.py:112
  119.8 1.8 convolution_multiply_fusion
  121.6 67.6 %psum.7 = f32[32,32]{0,1:T(8,128)S(1)} all-reduce(f32[32,32]{0,1:T(8,128)S(1)} %convolution_multiply_fusion), channel_id=1, replica_groups=mesh['hi'=16,'lo'=8] {'hi','lo'}, use_global_device_ids=true, to_apply=%region_0.1 | all-reduce | flops 1024 | bytes 8192 | tf_op jit(solution)/shard_map/psum | solution.py:116
  189.2 0.1 copy.35
  189.3 2.9 %cholesky.17 = f32[32,32]{1,0:T(8,128)S(1)} custom-call(f32[32,32]{1,0:T(8,128)S(1)} %fusion.138), custom_call_target="Cholesky" | custom-call | tf_op jit(solution)/shard_map/jit(cholesky)/cholesky | solution.py:117
  192.2 0.6 compare_reduce_fusion
  192.9 0.7 fusion.139
  193.5 2.4 %custom-call.7 = f32[1,32,32]{1,2,0:T(8,128)S(1)} custom-call(f32[1,32,32]{2,1,0:T(8,128)S(1)} %get-tuple-element.11), custom_call_target="InvertDiagBlocksLowerTriangular" | custom-call | tf_op jit(solution)/shard_map/jit(_solve_triangular)/triangular_solve | solution.py:118
  196.0 0.2 fusion.136
  196.2 3.2 %fusion.154 = f32[32,16384]{1,0:T(8,128)} fusion(f32[32,32]{1,0:T(8,128)S(1)} %fusion.136, f32[32,16384]{1,0:T(8,128)S(1)} %fusion.2), kind=kOutput, calls=%fused_computation.175 | convolution fusion | flops 201326592 | bytes 4198400 | tf_op jit(solution)/shard_map/dot_general | solution.py:121
  199.4 0.7 copy.36
  (16 shorter events, 0.1 us)
Async XLA Ops:
  3.8 11.5 %copy-start = (s32[20]{0:T(128)S(1)}, s32[20]{0:T(128)}, u32[]{:S(2)}) copy-start(s32[20]{0:T(128)} %param.7) | copy-start | bytes 244
  3.8 16.6 %copy-start.1 = (s32[21]{0:T(128)S(1)}, s32[21]{0:T(128)}, u32[]{:S(2)}) copy-start(s32[21]{0:T(128)} %param.6) | copy-start | bytes 256
  3.8 41.6 %all-to-all-start = ((f32[32,128,128]{2,0,1:T(8,128)}), f32[32,128,128]{2,0,1:T(8,128)S(1)}, u32[]{:S(2)}, u32[]{:S(2)}) async-start(f32[32,128,128]{2,0,1:T(8,128)} %copy_bitcast_fusion), calls=%async_computation | async-start | bytes 4194304 | tf_op jit(solution)/shard_map/all_to_all | solution.py:98
  55.5 54.7 %all-to-all-start.1 = ((f32[32,128,128]{2,0,1:T(8,128)}), f32[32,128,128]{2,0,1:T(8,128)}, u32[]{:S(2)}, u32[]{:S(2)}) async-start(f32[32,128,128]{2,0,1:T(8,128)} %copy.32), calls=%async_computation.1 | async-start | bytes 4194304 | tf_op jit(solution)/shard_map/all_to_all | solution.py:109
where the time goes:
time: 201 us; the launch traced here: 200 us
  blocking collectives  67.6 us (34%)
  other arithmetic  35.6 us (18%)
  waiting for transfers between devices  25 us (12%)
  between operations  20.7 us (10%)
  matrix products  18.7 us (9%)
  starting transfers between devices  17.4 us (9%)
  local copies, waits for them, and re-layouts  15.1 us (8%)
    psum x1, blocking collectives, local(): gram_matrix = lax.psum(local_gram, ('hi', 'lo'))  67.6 us
    all_to_all x1, waiting for transfers between devices, local(): lax.all_to_all(shaped, ('hi', 'lo'), split_axis=1, concat_axis=1, tiled=T...  25 us
    add x1, other arithmetic, local(): diagonal = diagonal + fields[site_number] * spin_value(site_number)  17.3 us
    all_to_all x1, starting transfers between devices, local(): lax.all_to_all(shaped, ('hi', 'lo'), split_axis=1, concat_axis=1, tiled=T...  11.5 us
    sub x1, other arithmetic, local(): filtered = 4.0 / site_count * (applied + remote_part) - previous  9.63 us
    all_to_all x1, starting transfers between devices, local(): lax.all_to_all(bond_terms.reshape(arrived.shape), ('hi', 'lo'), split_axi...  5.89 us
  transfers between devices with their start and end apart: 2, of which 1 were waited for; matrix products, arithmetic and copies ran while one was open for 17% of the time, Pallas kernels for 0%

commit v1 on v0

--- a/solution.py
+++ b/solution.py
@@ -113,7 +113,8 @@
     local_gram = jnp.dot(filtered, filtered.T, precision=lax.Precision.HIGHEST) / (
         amp_count * devices
     )
-    gram_matrix = lax.psum(local_gram, ("hi", "lo"))
+    shards = lax.all_gather(local_gram, ("hi", "lo"))
+    gram_matrix = jnp.sum(shards, axis=0)
     lower_factor = jnp.linalg.cholesky(gram_matrix)
     inverse = jax.scipy.linalg.solve_triangular(
         lower_factor, jnp.eye(vectors, dtype=jnp.float32), lower=True

time: 201 us -> 177 us (0.88)
  blocking collectives: 67.6 us -> 42.1 us
    psum x1 -> x0, blocking collectives: 67.6 us -> none  [local(): gram_matrix = lax.psum(local_gram, ('hi', 'lo'))]
    all_gather x0 -> x1, blocking collectives: none -> 42.1 us  [local(): shards = lax.all_gather(local_gram, ('hi', 'lo'))]
  transfers between devices with their start and end apart: 2 -> 2, of which waited for: 1 -> 1; matrix products, arithmetic and copies ran while one was open for 17% -> 19% of each run, Pallas kernels for 0% -> 0%
where the time goes in v1:
time: 177 us; the launch traced here: 176 us
  blocking collectives  42.1 us (24%)
  other arithmetic  37.4 us (21%)
  waiting for transfers between devices  25 us (14%)
  between operations  20.7 us (12%)
  matrix products  18.7 us (11%)
  starting transfers between devices  17.4 us (10%)
  local copies, waits for them, and re-layouts  15.1 us (9%)
    all_gather x1, blocking collectives, local(): shards = lax.all_gather(local_gram, ('hi', 'lo'))  42.1 us
    all_to_all x1, waiting for transfers between devices, local(): lax.all_to_all(shaped, ('hi', 'lo'), split_axis=1, concat_axis=1, tiled=T...  25 us
    add x1, other arithmetic, local(): diagonal = diagonal + fields[site_number] * spin_value(site_number)  17.3 us
    all_to_all x1, starting transfers between devices, local(): lax.all_to_all(shaped, ('hi', 'lo'), split_axis=1, concat_axis=1, tiled=T...  11.5 us
    sub x1, other arithmetic, local(): filtered = 4.0 / site_count * (applied + remote_part) - previous  9.63 us
    all_to_all x1, starting transfers between devices, local(): lax.all_to_all(bond_terms.reshape(arrived.shape), ('hi', 'lo'), split_axi...  5.89 us
    another operation x3, other arithmetic, local(): lower_factor = jnp.linalg.cholesky(gram_matrix)  3.59 us
  transfers between devices with their start and end apart: 2, of which 1 were waited for; matrix products, arithmetic and copies ran while one was open for 19% of the time, Pallas kernels for 0%

profile of v1, /device:TPU:1, one launch (start us, length us, event | category | flops | bytes accessed | tf_op | source)
XLA Modules:
  0.0 176.4 jit_solution(8006622952608969433)
XLA Ops:
  0.6 3.2 %copy_bitcast_fusion = f32[32,128,128]{2,0,1:T(8,128)} fusion(f32[32,16384]{1,0:T(8,128)} %param.5), kind=kLoop, calls=%fused_computation.6 | loop fusion | bytes 4194304 | tf_op jit(solution)/shard_map/reshape | solution.py:77
  3.8 0.0 copy-start
  3.8 0.0 copy-start.1
  3.8 11.5 %all-to-all-start = ((f32[32,128,128]{2,0,1:T(8,128)}), f32[32,128,128]{2,0,1:T(8,128)S(1)}, u32[]{:S(2)}, u32[]{:S(2)}) async-start(f32[32,128,128]{2,0,1:T(8,128)} %copy_bitcast_fusion), calls=%async_computation | async-start | bytes 4194304 | tf_op jit(solution)/shard_map/all_to_all | solution.py:98
  15.3 0.0 copy-done
  15.4 0.7 fusion.153
  20.4 0.0 copy-done.1
  20.4 25.0 %all-to-all-done = f32[32,128,128]{2,0,1:T(8,128)S(1)} async-done(((f32[32,128,128]{2,0,1:T(8,128)}), f32[32,128,128]{2,0,1:T(8,128)S(1)}, u32[]{:S(2)}, u32[]{:S(2)}) %all-to-all-start) | async-done | bytes 2097184 | tf_op jit(solution)/shard_map/all_to_all | solution.py:98
  45.4 2.3 %fusion.7 = f32[32,64,2,128]{3,1,2,0:T(8,128)S(1)} fusion(f32[32,64,2,128]{3,0,2,1:T(8,128)S(1)} %bitcast.130, s32[128]{0:T(128)S(1)} %iota_xor_fusion), kind=kOutput, calls=%fused_computation.14 | convolution fusion | flops 805322752 | bytes 4194816 | tf_op jit(solution)/shard_map/vatbl,lj->vatbj/dot_general | solution.py:26
  47.7 0.3 multiply_multiply_fusion
  48.1 1.7 copy.28
  49.8 3.2 %bitcast_add_fusion.3 = f32[32,128,128]{2,1,0:T(8,128)S(1)} fusion(f32[32,128,128]{2,1,0:T(8,128)S(1)} %bitcast.135, f32[32,128,128]{2,0,1:T(8,128)S(1)} %all-to-all-done, f32[]{:T(128)S(6)} %mul.670, f32[]{:T(128)S(6)} %mul.669, f32[]{:T(128)S(6)} %mul.668, f32[]{:T(128)S(6)} %mul.667, f32[]{:T(128)S(6)} %mul.666, f32[]{:T(128)S(6)} %mul.665, ...), kind=kOutput, calls=%fused_computation.7 | convolution fusion | flops 806207488 | bytes 6295320 | tf_op jit(solution)/shard_map/vtl,tu->vul/dot_general | solution.py:100
  53.0 2.5 %copy.29 = f32[32,128,128]{2,0,1:T(8,128)} copy(f32[32,128,128]{2,1,0:T(8,128)S(1)} %bitcast_add_fusion.3) | data formatting | bytes 4194304 | tf_op jit(solution)/shard_map/add | solution.py:108
  55.5 5.9 %all-to-all-start.1 = ((f32[32,128,128]{2,0,1:T(8,128)}), f32[32,128,128]{2,0,1:T(8,128)}, u32[]{:S(2)}, u32[]{:S(2)}) async-start(f32[32,128,128]{2,0,1:T(8,128)} %copy.29), calls=%async_computation.1 | async-start | bytes 4194304 | tf_op jit(solution)/shard_map/all_to_all | solution.py:109
  61.4 0.7 fusion.151
  74.1 2.0 %copy.37 = f32[4,8,128,128]{3,2,1,0:T(8,128)S(1)} copy(f32[4,8,128,128]{3,1,2,0:T(8,128)} %bitcast.129) | data formatting | bytes 4194304
  76.1 3.4 %convolution_bitcast_fusion.1 = f32[32,128,128]{1,2,0:T(8,128)} fusion(f32[32,128,128]{2,1,0:T(8,128)S(1)} %bitcast.126, f32[]{:T(128)S(6)} %mul.659, f32[]{:T(128)S(6)} %mul.658, f32[]{:T(128)S(6)} %mul.657, f32[]{:T(128)S(6)} %mul.656, f32[]{:T(128)S(6)} %mul.655, f32[]{:T(128)S(6)} %mul.654, s32[128]{0:T(128)S(1)} %get-tuple-element.52, ...), kind=kOutput, calls=%fused_computation.16 | convolution fusion | flops 805683200 | bytes 4198168 | tf_op jit(solution)/shard_map/vtl,lu->vtu/dot_general | solution.py:82
  79.5 2.9 %copy.24 = f32[32,128,128]{2,1,0:T(8,128)} copy(f32[32,128,128]{1,2,0:T(8,128)} %convolution_bitcast_fusion.1) | data formatting | bytes 4194304 | tf_op jit(solution)/shard_map/vtl,lu->vtu/dot_general | solution.py:82
  86.2 0.6 fusion.152
  86.7 17.3 %add_add_fusion = f32[16384]{0:T(1024)S(1)} fusion(f32[]{:T(128)S(6)} %mul.645, f32[]{:T(128)S(6)} %mul.644, f32[]{:T(128)S(6)} %mul.642, f32[]{:T(128)S(6)} %mul.641, f32[]{:T(128)S(6)} %mul.639, f32[]{:T(128)S(6)} %mul.638, f32[]{:T(128)S(6)} %mul.636, f32[]{:T(128)S(6)} %mul.635, f32[]{:T(128)S(6)} %mul.633, f32[]{:T(128)S(6)} %mul.632, f32[]{:T(128)S(6)} %mul.630, ...), kind=kLoop, calls=%fused_computation.63 | loop fusion | flops 2260992 | bytes 65704 | tf_op jit(solution)/shard_map/add | solution.py:59
  104.1 1.1 convolution_bitcast_fusion
  105.2 1.6 multiply_multiply_fusion.1
  106.8 3.4 %fusion.14 = f32[128,32,128]{2,0,1:T(8,128)} fusion(f32[32,128,128]{2,1,0:T(8,128)S(1)} %bitcast.128, f32[]{:T(128)S(6)} %mul.653, s32[128]{0:T(128)S(1)} %get-tuple-element.52, f32[]{:T(128)S(6)} %mul.652, s32[128]{0:T(128)S(1)} %get-tuple-element.53, f32[]{:T(128)S(6)} %mul.651, s32[128]{0:T(128)S(1)} %get-tuple-element.54, f32[]{:T(128)S(6)} %mul.650, ...), kind=kOutput, calls=%fused_computation.20 | convolution fusion | flops 805683200 | bytes 4198168 | tf_op jit(solution)/shard_map/vtl,tu->vul/dot_general | solution.py:79
  110.2 0.0 all-to-all-done.1
  110.2 9.6 %fusion.2 = f32[32,16384]{1,0:T(8,128)S(1)} fusion(f32[32,16384]{1,0:T(8,128)} %param.4, f32[4,8,128,128]{3,2,1,0:T(8,128)} %bitcast.131, f32[4,8,128,128]{3,2,1,0:T(8,128)} %bitcast.133, f32[4,8,128,128]{3,2,1,0:T(8,128)} %bitcast.132, f32[32,16384]{1,0:T(8,128)} %param.5, f32[16384]{0:T(1024)S(1)} %add_add_fusion, f32[32,128,128]{2,0,1:T(8,128)} %all-to-all-done.1), kind=kLoop, calls=%fused_computation.3 | loop fusion | flops 3670016 | bytes 14745600 | tf_op jit(solution)/shard_map/sub | solution.py:112
  119.8 1.8 %convolution_multiply_fusion = f32[32,32]{1,0:T(8,128)S(1)} fusion(f32[32,16384]{1,0:T(8,128)S(1)} %fusion.2), kind=kOutput, calls=%fused_computation.17 | convolution fusion | flops 201327616 | bytes 2101248 | tf_op jit(solution)/shard_map/dot_general | solution.py:113
  121.6 42.1 %all-gather = f32[4096,32]{1,0:T(8,128)} all-gather(f32[32,32]{1,0:T(8,128)S(1)} %convolution_multiply_fusion), channel_id=2, replica_groups=mesh['hi'=16,'lo'=8] {'hi','lo'}, dimensions={0}, use_global_device_ids=true | all-gather | bytes 528384 | tf_op jit(solution)/shard_map/all_gather | solution.py:116
  163.7 1.8 %reduce_sum.9 = f32[32,32]{1,0:T(8,128)S(1)} reduce(f32[128,32,32]{2,1,0:T(8,128)} %bitcast.134, f32[]{:T(128)} %constant.106.clone.1), dimensions={0}, to_apply=%region_0.1 | reduce | flops 130048 | bytes 528388 | tf_op jit(solution)/shard_map/reduce_sum | solution.py:117
  165.5 0.1 copy.31
  165.5 2.9 %cholesky.17 = f32[32,32]{1,0:T(8,128)S(1)} custom-call(f32[32,32]{1,0:T(8,128)S(1)} %fusion.138), custom_call_target="Cholesky" | custom-call | tf_op jit(solution)/shard_map/jit(cholesky)/cholesky | solution.py:118
  168.5 0.6 compare_reduce_fusion
  169.1 0.7 fusion.139
  169.8 2.4 %custom-call.7 = f32[1,32,32]{1,2,0:T(8,128)S(1)} custom-call(f32[1,32,32]{2,1,0:T(8,128)S(1)} %get-tuple-element.11), custom_call_target="InvertDiagBlocksLowerTriangular" | custom-call | tf_op jit(solution)/shard_map/jit(_solve_triangular)/triangular_solve | solution.py:119
  172.2 0.2 fusion.136
  172.5 3.2 %fusion.154 = f32[32,16384]{1,0:T(8,128)} fusion(f32[32,32]{1,0:T(8,128)S(1)} %fusion.136, f32[32,16384]{1,0:T(8,128)S(1)} %fusion.2), kind=kOutput, calls=%fused_computation.175 | convolution fusion | flops 201326592 | bytes 4198400 | tf_op jit(solution)/shard_map/dot_general | solution.py:122
  175.7 0.7 copy.32
  (16 shorter events, 0.1 us)
Async XLA Ops:
  3.8 11.5 %copy-start = (s32[20]{0:T(128)S(1)}, s32[20]{0:T(128)}, u32[]{:S(2)}) copy-start(s32[20]{0:T(128)} %param.7) | copy-start | bytes 244
  3.8 16.6 %copy-start.1 = (s32[21]{0:T(128)S(1)}, s32[21]{0:T(128)}, u32[]{:S(2)}) copy-start(s32[21]{0:T(128)} %param.6) | copy-start | bytes 256
  3.8 41.6 %all-to-all-start = ((f32[32,128,128]{2,0,1:T(8,128)}), f32[32,128,128]{2,0,1:T(8,128)S(1)}, u32[]{:S(2)}, u32[]{:S(2)}) async-start(f32[32,128,128]{2,0,1:T(8,128)} %copy_bitcast_fusion), calls=%async_computation | async-start | bytes 4194304 | tf_op jit(solution)/shard_map/all_to_all | solution.py:98
  55.5 54.7 %all-to-all-start.1 = ((f32[32,128,128]{2,0,1:T(8,128)}), f32[32,128,128]{2,0,1:T(8,128)}, u32[]{:S(2)}, u32[]{:S(2)}) async-start(f32[32,128,128]{2,0,1:T(8,128)} %copy.29), calls=%async_computation.1 | async-start | bytes 4194304 | tf_op jit(solution)/shard_map/all_to_all | solution.py:109
